TPU v7x, 32 devices: a whole 2x2x4 slice. The times are simulated.
32 devices in a mesh: grp: 4 (over y, x), fsdp: 8 (over z, core).
Axes of the slice: x: 2, y: 2, z: 4, core: 2. Of those that a mesh axis runs over, the one named last changes fastest.
Arguments:
- tokens: bfloat16 [64, 4096], P(('grp', 'fsdp')), may hold values from -128 to 128
- norm_gain: float32 [4096], replicated, may hold values from 0.25 to 1.75
- routes: int32 [64, 8], P(('grp', 'fsdp')), may hold values from 0 to 31, all different within a row; in each aligned block of 16 rows (0 to 15, 16 to 31, ...) at most 8 rows name the same one
- gate_probs: bfloat16 [64, 8], P(('grp', 'fsdp')), may hold values from 0.019897461 to 1
- w_gate_up: bfloat16 [32, 4096, 2048], P(('grp', 'fsdp')), may hold values from -0.09375 to 0.09375
- w_down: bfloat16 [32, 1024, 4096], P(('grp', 'fsdp')), may hold values from -0.1875 to 0.1875
Outputs:
- moe_out: bfloat16 [64, 4096], P(('grp', 'fsdp'))
Inputs may be any that keep to these rules, and one draw needn't show every extreme that they name: `routes`: each row names 8 different experts. In every aligned block of 16 rows no expert is named by more than 8 rows, a bound that some block reaches.
All inputs are finite; a program needn't handle non-finite values.
Results may differ from a plain program's by a relative error of at most 0.0095.
Values may be sent and summed in bfloat16 or wider, within the bound.
No kernel may reach another device: no remote copies, remote signals or barrier semaphores. Data moves between devices by JAX's collectives and lax.ppermute only.
A program may use at most 64 MiB of HBM per device.

v0:
```python
import jax
import jax.numpy as jnp
from jax import lax
from jax.sharding import PartitionSpec as P

FF = 1024


def local(tokens, norm_gain, routes, gate_probs, w_gate_up, w_down):
    group_count = lax.axis_size("grp")
    shard_count = lax.axis_size("fsdp")
    shard_index = lax.axis_index("fsdp")
    hidden_dev = w_down.shape[1]
    split_count = FF // hidden_dev
    expert_count = group_count * shard_count // split_count
    rows_dev = tokens.shape[0]
    top_count = routes.shape[1]
    block_rows = rows_dev * shard_count
    capacity = 2 * rows_dev * shard_count * top_count // expert_count
    width = tokens.shape[1]
    as_float = tokens.astype(jnp.float32)
    mean_square = jnp.mean(as_float * as_float, axis=-1, keepdims=True)
    normed = (as_float * lax.rsqrt(mean_square + 1e-06) * norm_gain).astype(jnp.bfloat16)
    rows_all, probs_all = (
        lax.all_gather(normed, "fsdp", axis=0, tiled=True),
        lax.all_gather(gate_probs, "fsdp", axis=0, tiled=True),
    )
    routes_all = lax.all_gather(routes, "fsdp", axis=0, tiled=True)
    probs = probs_all.astype(jnp.float32)
    combine = probs / jnp.sum(probs, axis=-1, keepdims=True)
    targets = (
        jnp.arange(group_count, dtype=jnp.int32) * (shard_count // split_count)
        + shard_index // split_count
    )
    matched = routes_all[None, :, :] == targets[:, None, None]
    is_routed = jnp.any(matched, axis=-1)
    row_weight = jnp.sum(jnp.where(matched, combine[None, :, :], 0.0), axis=-1)
    slot_index = jnp.cumsum(is_routed.astype(jnp.int32), axis=1) - 1
    select = (
        slot_index[:, None, :] == jnp.arange(capacity, dtype=jnp.int32)[None, :, None]
    ) & is_routed[:, None, :]
    outgoing = jnp.einsum(
        "gcb,bd->gcd", select.astype(jnp.bfloat16), rows_all, preferred_element_type=jnp.float32
    ).astype(jnp.bfloat16)
    incoming = lax.all_to_all(outgoing, "grp", split_axis=0, concat_axis=0, tiled=True)
    flattened = incoming.reshape(-1, width)
    projected = jnp.dot(flattened, w_gate_up[0], preferred_element_type=jnp.float32)
    hidden = (jax.nn.silu(projected[:, :hidden_dev]) * projected[:, hidden_dev:]).astype(
        jnp.bfloat16
    )
    result = jnp.dot(hidden, w_down[0], preferred_element_type=jnp.float32).astype(jnp.bfloat16)
    returned = lax.all_to_all(
        result.reshape(incoming.shape), "grp", split_axis=0, concat_axis=0, tiled=True
    )
    mix_matrix = (select.astype(jnp.float32) * row_weight[:, None, :]).reshape(-1, block_rows)
    row_partial = jnp.dot(
        mix_matrix.T,
        returned.reshape(-1, width),
        precision=lax.Precision.HIGHEST,
        preferred_element_type=jnp.float32,
    )
    summed = lax.psum_scatter(row_partial, "fsdp", scatter_dimension=0, tiled=True)
    return summed.astype(jnp.bfloat16)


def solution(mesh):
    return jax.shard_map(
        local,
        mesh=mesh,
        in_specs=(
            P(("grp", "fsdp"), None),
            P(),
            P(("grp", "fsdp"), None),
            P(("grp", "fsdp"), None),
            P(("grp", "fsdp"), None, None),
            P(("grp", "fsdp"), None, None),
        ),
        out_specs=P(("grp", "fsdp"), None),
        check_vma=False,
    )
```

profile of v0, /device:TPU:0, one launch (start us, length us, event | category | flops | bytes accessed | tf_op | source)
XLA Modules:
  0.0 94.8 jit_solution(7591240734302826050)
XLA Ops:
  0.0 0.9 fusion.14
  0.9 13.7 %all-gather = s32[8,2,8]{2,1,0:T(2,128)S(1)} all-gather(s32[1,2,8]{2,1,0:T(2,128)} %bitcast.29), channel_id=1, replica_groups=mesh['grp'=4,'fsdp'=8] {'fsdp'}, dimensions={0}, use_global_device_ids=true | all-gather | bytes 576 | tf_op jit(solution)/shard_map/all_gather | solution.py:28
  14.6 0.1 copy.7
  14.6 0.1 compare_reduce_fusion
  14.7 0.2 reduce_window_sum.11
  14.9 0.8 fusion.19
  15.7 14.0 %all-gather.2 = bf16[8,2,4096]{2,1,0:T(2,128)(2,1)S(1)} all-gather(bf16[1,2,4096]{2,1,0:T(2,128)(2,1)S(1)} %fusion.19), channel_id=1, replica_groups=mesh['grp'=4,'fsdp'=8] {'fsdp'}, dimensions={0}, use_global_device_ids=true | all-gather | bytes 147456 | tf_op jit(solution)/shard_map/all_gather | solution.py:25
  29.7 0.1 reshape.46
  29.8 0.9 convolution_convert_fusion
  30.7 3.7 %all-to-all-start = ((bf16[4,8,4096]{2,1,0:T(8,128)(2,1)}), bf16[4,8,4096]{2,1,0:T(8,128)(2,1)S(1)}, u32[]{:S(2)}, u32[]{:S(2)}) async-start(bf16[4,8,4096]{2,1,0:T(8,128)(2,1)} %convolution_convert_fusion), calls=%async_computation | async-start | bytes 524288 | tf_op jit(solution)/shard_map/all_to_all | solution.py:45
  34.4 8.8 %all-gather.1 = bf16[8,2,8]{2,1,0:T(2,128)(2,1)S(1)} all-gather(bf16[1,2,8]{2,1,0:T(2,128)(2,1)} %bitcast.30), channel_id=1, replica_groups=mesh['grp'=4,'fsdp'=8] {'fsdp'}, dimensions={0}, use_global_device_ids=true | all-gather | bytes 288 | tf_op jit(solution)/shard_map/all_gather | solution.py:26
  43.2 0.1 convert_reduce_fusion
  43.3 0.1 reshape.45
  43.4 0.0 copy-start.1
  43.4 0.0 all-to-all-done
  43.4 0.0 copy-start
  43.4 8.9 %fusion = f32[32,2048]{1,0:T(8,128)S(1)} fusion(bf16[1,4096,2048]{2,1,0:T(8,128)(2,1)} %param.10, bf16[4,8,4096]{2,1,0:T(8,128)(2,1)S(1)} %all-to-all-done), kind=kOutput, calls=%fused_computation | convolution fusion | flops 536870912 | bytes 17301504 | tf_op jit(solution)/shard_map/dot_general | solution.py:47
  52.3 0.0 copy-done
  52.3 2.2 %fusion.7 = bf16[4,8,4096]{2,1,0:T(8,128)(2,1)} fusion(bf16[1,1024,4096]{2,1,0:T(8,128)(2,1)S(1)} %copy-done, f32[32,2048]{1,0:T(8,128)S(1)} %fusion), kind=kOutput, calls=%fused_computation.6 | convolution fusion | flops 268763136 | bytes 8912896 | tf_op jit(solution)/shard_map/dot_general | solution.py:51
  54.5 4.2 %all-to-all-start.1 = ((bf16[4,8,4096]{2,1,0:T(8,128)(2,1)}), bf16[4,8,4096]{2,1,0:T(8,128)(2,1)S(1)}, u32[]{:S(2)}, u32[]{:S(2)}) async-start(bf16[4,8,4096]{2,1,0:T(8,128)(2,1)} %fusion.7), calls=%async_computation.1 | async-start | bytes 524288 | tf_op jit(solution)/shard_map/all_to_all | solution.py:52
  58.7 0.1 broadcast_divide_fusion
  58.8 0.1 copy.8
  58.9 0.0 copy-done.1
  58.9 0.6 dynamic-slice
  60.1 0.1 fusion.17
  60.2 4.4 %all-to-all-done.1 = bf16[4,8,4096]{2,1,0:T(8,128)(2,1)S(1)} async-done(((bf16[4,8,4096]{2,1,0:T(8,128)(2,1)}), bf16[4,8,4096]{2,1,0:T(8,128)(2,1)S(1)}, u32[]{:S(2)}, u32[]{:S(2)}) %all-to-all-start.1) | async-done | bytes 262176 | tf_op jit(solution)/shard_map/all_to_all | solution.py:52
  64.6 0.3 convolution_bitcast_fusion
  64.9 29.2 %all-reduce.2 = bf16[16,4096]{1,0:T(8,128)(2,1)S(1)} all-reduce(f32[16,4096]{1,0:T(8,128)S(1)} %convolution_bitcast_fusion), channel_id=2, replica_groups=mesh['grp'=4,'fsdp'=8] {'fsdp'}, use_global_device_ids=true, to_apply=%region_5.6.clone | all-reduce | flops 65536 | bytes 393216
  94.1 0.6 dynamic-slice_convert_fusion
  (4 shorter events, 0.0 us)
Async XLA Ops:
  30.7 12.7 %all-to-all-start = ((bf16[4,8,4096]{2,1,0:T(8,128)(2,1)}), bf16[4,8,4096]{2,1,0:T(8,128)(2,1)S(1)}, u32[]{:S(2)}, u32[]{:S(2)}) async-start(bf16[4,8,4096]{2,1,0:T(8,128)(2,1)} %convolution_convert_fusion), calls=%async_computation | async-start | bytes 524288 | tf_op jit(solution)/shard_map/all_to_all | solution.py:45
  43.4 15.5 %copy-start.1 = (u32[32]{0:T(128)S(1)}, u32[32]{0:T(128)}, u32[]{:S(2)}) copy-start(u32[32]{0:T(128)} %constant.44) | copy-start | bytes 388
  43.4 8.9 %copy-start = (bf16[1,1024,4096]{2,1,0:T(8,128)(2,1)S(1)}, bf16[1,1024,4096]{2,1,0:T(8,128)(2,1)}, u32[]{:S(2)}) copy-start(bf16[1,1024,4096]{2,1,0:T(8,128)(2,1)} %param.11) | copy-start | bytes 25165828
  54.5 10.0 %all-to-all-start.1 = ((bf16[4,8,4096]{2,1,0:T(8,128)(2,1)}), bf16[4,8,4096]{2,1,0:T(8,128)(2,1)S(1)}, u32[]{:S(2)}, u32[]{:S(2)}) async-start(bf16[4,8,4096]{2,1,0:T(8,128)(2,1)} %fusion.7), calls=%async_computation.1 | async-start | bytes 524288 | tf_op jit(solution)/shard_map/all_to_all | solution.py:52
where the time goes:
time: 95.3 us; the launch traced here: 94.8 us
  blocking collectives  65.7 us (69%)
  matrix products  12.4 us (13%)
  starting transfers between devices  7.91 us (8%)
  waiting for transfers between devices  4.35 us (5%)
  other arithmetic  2.24 us (2%)
  local copies, waits for them, and re-layouts  1.5 us (2%)
    unnamed x1, blocking collectives  29.2 us
    all_gather x1, blocking collectives, local(): lax.all_gather(normed, 'fsdp', axis=0, tiled=True)  14 us
    all_gather x1, blocking collectives, local(): routes_all = lax.all_gather(routes, 'fsdp', axis=0, tiled=True)  13.7 us
    dot_general x1, matrix products, local(): jnp.dot(flattened, w_gate_up[0], preferred_element_type=jnp.float32)  8.9 us
    all_gather x1, blocking collectives, local(): lax.all_gather(gate_probs, 'fsdp', axis=0, tiled=True)  8.82 us
    all_to_all x1, waiting for transfers between devices, local(): lax.all_to_all(result.reshape(incoming.shape), 'grp', split_axis=0, conca...  4.35 us
    all_to_all x1, starting transfers between devices, local(): lax.all_to_all(result.reshape(incoming.shape), 'grp', split_axis=0, conca...  4.19 us
    all_to_all x1, starting transfers between devices, local(): lax.all_to_all(outgoing, 'grp', split_axis=0, concat_axis=0, tiled=True)  3.71 us
  transfers between devices with their start and end apart: 2, of which 1 were waited for; matrix products, arithmetic and copies ran while one was open for 1% of the time, Pallas kernels for 0%

commit v1 on v0

--- a/solution.py
+++ b/solution.py
@@ -4,6 +4,19 @@
 from jax.sharding import PartitionSpec as P
 
 FF = 1024
+
+
+def gather_around(x, axis, dim):
+    ways = lax.axis_size(axis)
+    up = [(d, (d + 1) % ways) for d in range(ways)]
+    down = [(d, (d - 1) % ways) for d in range(ways)]
+    earlier, later = ([x], [x])
+    for _ in range(ways // 2):
+        earlier.append(lax.ppermute(earlier[-1], axis, up))
+    for _ in range((ways - 1) // 2):
+        later.append(lax.ppermute(later[-1], axis, down))
+    line = jnp.concatenate([*earlier[::-1], *later[1:]], axis=dim)
+    return jnp.roll(line, (lax.axis_index(axis) - ways // 2) * x.shape[dim], axis=dim)
 
 
 def local(tokens, norm_gain, routes, gate_probs, w_gate_up, w_down):
@@ -23,7 +36,7 @@
     normed = (as_float * lax.rsqrt(mean_square + 1e-06) * norm_gain).astype(jnp.bfloat16)
     rows_all, probs_all = (
         lax.all_gather(normed, "fsdp", axis=0, tiled=True),
-        lax.all_gather(gate_probs, "fsdp", axis=0, tiled=True),
+        gather_around(gate_probs, "fsdp", 0),
     )
     routes_all = lax.all_gather(routes, "fsdp", axis=0, tiled=True)
     probs = probs_all.astype(jnp.float32)

time: 95.3 us -> 106 us (1.11)
  starting transfers between devices: 7.91 us -> 18.5 us
  blocking collectives: 65.7 us -> 56.6 us
  waiting for transfers between devices: 4.35 us -> 12.6 us
  local copies, waits for them, and re-layouts: 1.5 us -> 2.84 us
    ppermute x0 -> x7, starting transfers between devices: none -> 10.6 us  [the longest x3 10.5 us: gather_around(): later.append(lax.ppermute(later[-1], axis, down))]
    all_gather x1 -> x0, blocking collectives: 8.82 us -> none  [local(): lax.all_gather(gate_probs, 'fsdp', axis=0, tiled=True)]
    ppermute x0 -> x7, waiting for transfers between devices: none -> 7.38 us  [the longest x4 7.28 us: gather_around(): earlier.append(lax.ppermute(earlier[-1], axis, up))]
    unnamed x7 -> x6, local copies, waits for them, and re-layouts: 0.72 us -> 2.1 us
  transfers between devices with their start and end apart: 2 -> 9, of which waited for: 1 -> 4; matrix products, arithmetic and copies ran while one was open for 1% -> 2% of each run, Pallas kernels for 0% -> 0%
where the time goes in v1:
time: 106 us
  blocking collectives  56.6 us (53%)
  starting transfers between devices  18.5 us (17%)
  waiting for transfers between devices  12.6 us (12%)
  matrix products  12.4 us (12%)
  local copies, waits for them, and re-layouts  2.84 us (3%)
  other arithmetic  2.25 us (2%)
    unnamed x1, blocking collectives  29 us
    all_gather x1, blocking collectives, local(): lax.all_gather(normed, 'fsdp', axis=0, tiled=True)  14 us
    all_gather x1, blocking collectives, local(): routes_all = lax.all_gather(routes, 'fsdp', axis=0, tiled=True)  13.7 us
    ppermute x3, starting transfers between devices, gather_around(): later.append(lax.ppermute(later[-1], axis, down))  10.5 us
    dot_general x1, matrix products, local(): jnp.dot(flattened, w_gate_up[0], preferred_element_type=jnp.float32)  8.9 us
    ppermute x4, waiting for transfers between devices, gather_around(): earlier.append(lax.ppermute(earlier[-1], axis, up))  7.28 us
    all_to_all x1, waiting for transfers between devices, local(): lax.all_to_all(result.reshape(incoming.shape), 'grp', split_axis=0, conca...  5.21 us
    all_to_all x1, starting transfers between devices, local(): lax.all_to_all(result.reshape(incoming.shape), 'grp', split_axis=0, conca...  4.19 us
  transfers between devices with their start and end apart: 9, of which 4 were waited for; matrix products, arithmetic and copies ran while one was open for 2% of the time, Pallas kernels for 0%

profile of v1, /device:TPU:0, one launch (start us, length us, event | category | flops | bytes accessed | tf_op | source)
XLA Modules:
  0.0 105.9 jit_solution(17942365301292912977)
XLA Ops:
  0.0 13.7 %all-gather = s32[8,2,8]{2,1,0:T(2,128)S(1)} all-gather(s32[1,2,8]{2,1,0:T(2,128)} %bitcast.25), channel_id=1, replica_groups=mesh['grp'=4,'fsdp'=8] {'fsdp'}, dimensions={0}, use_global_device_ids=true | all-gather | bytes 576 | tf_op jit(solution)/shard_map/all_gather | solution.py:41
  13.7 0.1 copy.12
  13.7 0.1 compare_reduce_fusion
  13.8 0.2 reduce_window_sum.11
  14.0 0.9 fusion.14
  14.9 0.8 fusion.19
  15.7 14.0 %all-gather.1 = bf16[8,2,4096]{2,1,0:T(2,128)(2,1)S(1)} all-gather(bf16[1,2,4096]{2,1,0:T(2,128)(2,1)S(1)} %fusion.19), channel_id=1, replica_groups=mesh['grp'=4,'fsdp'=8] {'fsdp'}, dimensions={0}, use_global_device_ids=true | all-gather | bytes 147456 | tf_op jit(solution)/shard_map/all_gather | solution.py:38
  29.7 0.1 reshape.42
  29.8 0.9 convolution_convert_fusion
  30.7 3.7 %all-to-all-start = ((bf16[4,8,4096]{2,1,0:T(8,128)(2,1)}), bf16[4,8,4096]{2,1,0:T(8,128)(2,1)S(1)}, u32[]{:S(2)}, u32[]{:S(2)}) async-start(bf16[4,8,4096]{2,1,0:T(8,128)(2,1)} %convolution_convert_fusion), calls=%async_computation | async-start | bytes 524288 | tf_op jit(solution)/shard_map/all_to_all | solution.py:58
  34.4 0.7 copy.13
  35.1 0.1 collective-permute-start
  35.2 3.5 %collective-permute-start.4 = (bf16[2,8]{0,1:T(8,128)(2,1)S(1)}, bf16[2,8]{0,1:T(8,128)(2,1)S(1)}, u32[]{:S(2)}, u32[]{:S(2)}) collective-permute-start(bf16[2,8]{0,1:T(8,128)(2,1)S(1)} %copy.13), channel_id=1, source_target_pairs={{0,7},{1,0},{2,1},{3,2},{4,3},{5,4},{6,5},{7,6},{8,15},{9,8},{10,9... | collective-permute-start | bytes 104 | tf_op jit(solution)/shard_map/ppermute | solution.py:17
  38.7 1.2 %dynamic-slice = u32[1]{0:T(128)} dynamic-slice(u32[32]{0:T(128)} %constant.70, u32[]{:T(128)S(6)} %add.48), dynamic_slice_sizes={1} | dynamic-slice | bytes 12
  40.5 0.0 collective-permute-done
  40.6 0.1 collective-permute-start.1
  40.6 0.0 collective-permute-done.4
  40.6 3.5 %collective-permute-start.5 = (bf16[2,8]{0,1:T(8,128)(2,1)S(1)}, bf16[2,8]{0,1:T(8,128)(2,1)S(1)}, u32[]{:S(2)}, u32[]{:S(2)}) collective-permute-start(bf16[2,8]{0,1:T(8,128)(2,1)S(1)} %collective-permute-done.4), channel_id=1, source_target_pairs={{0,7},{1,0},{2,1},{3,2},{4,3},{5,4},{6,5},{7,6},{8,15},{9,8},{10,9... | collective-permute-start | bytes 104 | tf_op jit(solution)/shard_map/ppermute | solution.py:17
  44.2 1.3 %collective-permute-done.1 = bf16[2,8]{0,1:T(8,128)(2,1)S(1)} collective-permute-done((bf16[2,8]{0,1:T(8,128)(2,1)S(1)}, bf16[2,8]{0,1:T(8,128)(2,1)S(1)}, u32[]{:S(2)}, u32[]{:S(2)}) %collective-permute-start.1) | collective-permute-done | bytes 64 | tf_op jit(solution)/shard_map/ppermute | solution.py:15
  45.4 0.0 collective-permute-start.2
  45.4 0.0 collective-permute-done.5
  45.5 3.5 %collective-permute-start.6 = (bf16[2,8]{0,1:T(8,128)(2,1)S(1)}, bf16[2,8]{0,1:T(8,128)(2,1)S(1)}, u32[]{:S(2)}, u32[]{:S(2)}) collective-permute-start(bf16[2,8]{0,1:T(8,128)(2,1)S(1)} %collective-permute-done.5), channel_id=1, source_target_pairs={{0,7},{1,0},{2,1},{3,2},{4,3},{5,4},{6,5},{7,6},{8,15},{9,8},{10,9... | collective-permute-start | bytes 104 | tf_op jit(solution)/shard_map/ppermute | solution.py:17
  49.0 1.3 %collective-permute-done.2 = bf16[2,8]{0,1:T(8,128)(2,1)S(1)} collective-permute-done((bf16[2,8]{0,1:T(8,128)(2,1)S(1)}, bf16[2,8]{0,1:T(8,128)(2,1)S(1)}, u32[]{:S(2)}, u32[]{:S(2)}) %collective-permute-start.2) | collective-permute-done | bytes 64 | tf_op jit(solution)/shard_map/ppermute | solution.py:15
  50.2 0.0 collective-permute-start.3
  50.2 0.0 collective-permute-done.6
  50.3 4.8 %collective-permute-done.3 = bf16[2,8]{0,1:T(8,128)(2,1)S(1)} collective-permute-done((bf16[2,8]{0,1:T(8,128)(2,1)S(1)}, bf16[2,8]{0,1:T(8,128)(2,1)S(1)}, u32[]{:S(2)}, u32[]{:S(2)}) %collective-permute-start.3) | collective-permute-done | bytes 64 | tf_op jit(solution)/shard_map/ppermute | solution.py:15
  55.0 0.1 concatenate.6
  55.1 0.1 convert_reduce_fusion
  55.2 0.0 all-to-all-done
  55.2 0.0 copy-start
  55.2 8.9 %fusion = f32[32,2048]{1,0:T(8,128)S(1)} fusion(bf16[1,4096,2048]{2,1,0:T(8,128)(2,1)} %param.10, bf16[4,8,4096]{2,1,0:T(8,128)(2,1)S(1)} %all-to-all-done), kind=kOutput, calls=%fused_computation | convolution fusion | flops 536870912 | bytes 17301504 | tf_op jit(solution)/shard_map/dot_general | solution.py:60
  64.1 0.0 copy-done
  64.1 2.2 %fusion.7 = bf16[4,8,4096]{2,1,0:T(8,128)(2,1)} fusion(bf16[1,1024,4096]{2,1,0:T(8,128)(2,1)S(1)} %copy-done, f32[32,2048]{1,0:T(8,128)S(1)} %fusion), kind=kOutput, calls=%fused_computation.6 | convolution fusion | flops 268763136 | bytes 8912896 | tf_op jit(solution)/shard_map/dot_general | solution.py:64
  66.4 4.2 %all-to-all-start.1 = ((bf16[4,8,4096]{2,1,0:T(8,128)(2,1)}), bf16[4,8,4096]{2,1,0:T(8,128)(2,1)S(1)}, u32[]{:S(2)}, u32[]{:S(2)}) async-start(bf16[4,8,4096]{2,1,0:T(8,128)(2,1)} %fusion.7), calls=%async_computation.1 | async-start | bytes 524288 | tf_op jit(solution)/shard_map/all_to_all | solution.py:65
  70.6 0.1 convert_divide_fusion
  70.6 0.1 fusion.17
  70.7 5.2 %all-to-all-done.1 = bf16[4,8,4096]{2,1,0:T(8,128)(2,1)S(1)} async-done(((bf16[4,8,4096]{2,1,0:T(8,128)(2,1)}), bf16[4,8,4096]{2,1,0:T(8,128)(2,1)S(1)}, u32[]{:S(2)}, u32[]{:S(2)}) %all-to-all-start.1) | async-done | bytes 262176 | tf_op jit(solution)/shard_map/all_to_all | solution.py:65
  75.9 0.3 convolution_bitcast_fusion
  76.3 29.0 %all-reduce.2 = bf16[16,4096]{1,0:T(8,128)(2,1)S(1)} all-reduce(f32[16,4096]{1,0:T(8,128)S(1)} %convolution_bitcast_fusion), channel_id=2, replica_groups=mesh['grp'=4,'fsdp'=8] {'fsdp'}, use_global_device_ids=true, to_apply=%region_5.6.clone | all-reduce | flops 65536 | bytes 393216
  105.2 0.6 dynamic-slice_convert_fusion
  (4 shorter events, 0.0 us)
Async XLA Ops:
  30.7 24.6 %all-to-all-start = ((bf16[4,8,4096]{2,1,0:T(8,128)(2,1)}), bf16[4,8,4096]{2,1,0:T(8,128)(2,1)S(1)}, u32[]{:S(2)}, u32[]{:S(2)}) async-start(bf16[4,8,4096]{2,1,0:T(8,128)(2,1)} %convolution_convert_fusion), calls=%async_computation | async-start | bytes 524288 | tf_op jit(solution)/shard_map/all_to_all | solution.py:58
  35.1 5.4 %collective-permute-start = (bf16[2,8]{0,1:T(8,128)(2,1)S(1)}, bf16[2,8]{0,1:T(8,128)(2,1)S(1)}, u32[]{:S(2)}, u32[]{:S(2)}) collective-permute-start(bf16[2,8]{0,1:T(8,128)(2,1)S(1)} %copy.13), channel_id=1, source_target_pairs={{0,1},{1,2},{2,3},{3,4},{4,5},{5,6},{6,7},{7,0},{8,9},{9,10},{10,1... | collective-permute-start | bytes 104 | tf_op jit(solution)/shard_map/ppermute | solution.py:15
  35.2 5.5 %collective-permute-start.4 = (bf16[2,8]{0,1:T(8,128)(2,1)S(1)}, bf16[2,8]{0,1:T(8,128)(2,1)S(1)}, u32[]{:S(2)}, u32[]{:S(2)}) collective-permute-start(bf16[2,8]{0,1:T(8,128)(2,1)S(1)} %copy.13), channel_id=1, source_target_pairs={{0,7},{1,0},{2,1},{3,2},{4,3},{5,4},{6,5},{7,6},{8,15},{9,8},{10,9... | collective-permute-start | bytes 104 | tf_op jit(solution)/shard_map/ppermute | solution.py:17
  40.6 4.9 %collective-permute-start.1 = (bf16[2,8]{0,1:T(8,128)(2,1)S(1)}, bf16[2,8]{0,1:T(8,128)(2,1)S(1)}, u32[]{:S(2)}, u32[]{:S(2)}) collective-permute-start(bf16[2,8]{0,1:T(8,128)(2,1)S(1)} %collective-permute-done), channel_id=1, source_target_pairs={{0,1},{1,2},{2,3},{3,4},{4,5},{5,6},{6,7},{7,0},{8,9},{9,10},{10,1... | collective-permute-start | bytes 104 | tf_op jit(solution)/shard_map/ppermute | solution.py:15
  40.6 4.8 %collective-permute-start.5 = (bf16[2,8]{0,1:T(8,128)(2,1)S(1)}, bf16[2,8]{0,1:T(8,128)(2,1)S(1)}, u32[]{:S(2)}, u32[]{:S(2)}) collective-permute-start(bf16[2,8]{0,1:T(8,128)(2,1)S(1)} %collective-permute-done.4), channel_id=1, source_target_pairs={{0,7},{1,0},{2,1},{3,2},{4,3},{5,4},{6,5},{7,6},{8,15},{9,8},{10,9... | collective-permute-start | bytes 104 | tf_op jit(solution)/shard_map/ppermute | solution.py:17
  45.4 4.8 %collective-permute-start.2 = (bf16[2,8]{0,1:T(8,128)(2,1)S(1)}, bf16[2,8]{0,1:T(8,128)(2,1)S(1)}, u32[]{:S(2)}, u32[]{:S(2)}) collective-permute-start(bf16[2,8]{0,1:T(8,128)(2,1)S(1)} %collective-permute-done.1), channel_id=1, source_target_pairs={{0,1},{1,2},{2,3},{3,4},{4,5},{5,6},{6,7},{7,0},{8,9},{9,10},{10,1... | collective-permute-start | bytes 104 | tf_op jit(solution)/shard_map/ppermute | solution.py:15
  45.5 4.8 %collective-permute-start.6 = (bf16[2,8]{0,1:T(8,128)(2,1)S(1)}, bf16[2,8]{0,1:T(8,128)(2,1)S(1)}, u32[]{:S(2)}, u32[]{:S(2)}) collective-permute-start(bf16[2,8]{0,1:T(8,128)(2,1)S(1)} %collective-permute-done.5), channel_id=1, source_target_pairs={{0,7},{1,0},{2,1},{3,2},{4,3},{5,4},{6,5},{7,6},{8,15},{9,8},{10,9... | collective-permute-start | bytes 104 | tf_op jit(solution)/shard_map/ppermute | solution.py:17
  50.2 4.8 %collective-permute-start.3 = (bf16[2,8]{0,1:T(8,128)(2,1)S(1)}, bf16[2,8]{0,1:T(8,128)(2,1)S(1)}, u32[]{:S(2)}, u32[]{:S(2)}) collective-permute-start(bf16[2,8]{0,1:T(8,128)(2,1)S(1)} %collective-permute-done.2), channel_id=1, source_target_pairs={{0,1},{1,2},{2,3},{3,4},{4,5},{5,6},{6,7},{7,0},{8,9},{9,10},{10,1... | collective-permute-start | bytes 104 | tf_op jit(solution)/shard_map/ppermute | solution.py:15
  55.2 8.9 %copy-start = (bf16[1,1024,4096]{2,1,0:T(8,128)(2,1)S(1)}, bf16[1,1024,4096]{2,1,0:T(8,128)(2,1)}, u32[]{:S(2)}) copy-start(bf16[1,1024,4096]{2,1,0:T(8,128)(2,1)} %param.11) | copy-start | bytes 25165828
  66.4 9.6 %all-to-all-start.1 = ((bf16[4,8,4096]{2,1,0:T(8,128)(2,1)}), bf16[4,8,4096]{2,1,0:T(8,128)(2,1)S(1)}, u32[]{:S(2)}, u32[]{:S(2)}) async-start(bf16[4,8,4096]{2,1,0:T(8,128)(2,1)} %fusion.7), calls=%async_computation.1 | async-start | bytes 524288 | tf_op jit(solution)/shard_map/all_to_all | solution.py:65
